TPU v7x, 256 devices: a whole 4x4x8 slice. The times are simulated.
256 devices in a mesh: cand: 32 (over y, z), tp: 8 (over x, core).
Axes of the slice: x: 4, y: 4, z: 8, core: 2. Of those that a mesh axis runs over, the one named last changes fastest.
Arguments:
- reward_query: bfloat16 [256, 32, 8192], P('cand', None, 'tp'), may hold values from -170 to 170
- reward_new: bfloat16 [256, 2, 32, 1024], P('cand', None, None, 'tp'), may hold values from -7 to 7
- reward_key_value_cache: bfloat16 [256, 2, 768, 1024], P('cand', None, None, 'tp'), may hold values from -6 to 6
- reward_length: int32 [256], P('cand'), may hold values from 1 to 768
- out_weight: bfloat16 [8192, 4096], P('tp'), may hold values from -0.09375 to 0.09375
- policy_cache: bfloat16 [256, 2, 768, 1024], P('cand', None, None, 'tp'), may hold values from -6 to 6
- policy_length: int32 [256], replicated, may hold values from 1 to 767
- source: int32 [128], replicated, may hold values from 0 to 255, as said below
- policy_query: bfloat16 [128, 8192], P('cand', 'tp'), may hold values from -170 to 170
- policy_new: bfloat16 [128, 2, 1024], P('cand', None, 'tp'), may hold values from -7 to 7
Outputs:
- reward_out: bfloat16 [8192, 4096], P('cand', 'tp')
- compacted: bfloat16 [128, 2, 768, 1024], P('cand', None, None, 'tp')
- policy_attn: bfloat16 [128, 8192], P('cand', 'tp')
Inputs may be any that keep to these rules, and one draw needn't show every extreme that they name: `source`: distinct candidate indices; the 8 candidates of each index of cand are named exactly 4 times.
All inputs are finite; a program needn't handle non-finite values.
Results may differ from a plain program's by a relative error of at most 0.0057.
Values may be sent and summed in bfloat16 or wider, within the bound.
A program may use at most 128 MiB of HBM per device.

v0:
```python
import jax
import jax.numpy as jnp
from jax import lax
from jax.sharding import PartitionSpec as P

ASKING_UNITS = 64
SHARED_KV_UNITS = 8
ATTN_DIM = 128
NEW_TOKEN_COUNT = 32
CACHE_LENGTH = 768


def body(
    reward_query,
    reward_new,
    reward_key_value_cache,
    reward_length,
    out_weight,
    policy_cache,
    policy_length,
    source,
    policy_query,
    policy_new,
):
    attention_clusters = ASKING_UNITS // SHARED_KV_UNITS
    score_scale = ATTN_DIM ** (-0.5)
    count = reward_query.shape[0]
    kv_heads = reward_key_value_cache.shape[-1] // ATTN_DIM
    head_list = reward_query.reshape(count, NEW_TOKEN_COUNT, kv_heads, attention_clusters, ATTN_DIM)
    cache_keys = reward_key_value_cache[:, 0].reshape(count, CACHE_LENGTH, kv_heads, ATTN_DIM)
    cache_values = reward_key_value_cache[:, 1].reshape(count, CACHE_LENGTH, kv_heads, ATTN_DIM)
    fresh_keys = reward_new[:, 0].reshape(count, NEW_TOKEN_COUNT, kv_heads, ATTN_DIM)
    fresh_values = reward_new[:, 1].reshape(count, NEW_TOKEN_COUNT, kv_heads, ATTN_DIM)
    old_scores = (
        jnp.einsum("ctkgd,cpkd->ckgtp", head_list, cache_keys, preferred_element_type=jnp.float32)
        * score_scale
    )
    new_scores = (
        jnp.einsum("ctkgd,cukd->ckgtu", head_list, fresh_keys, preferred_element_type=jnp.float32)
        * score_scale
    )
    cache_rows = lax.iota(jnp.int32, CACHE_LENGTH)
    old_visible = cache_rows[None, :] < reward_length[:, None]
    old_scores = jnp.where(old_visible[:, None, None, None, :], old_scores, -1e30)
    token_rows = lax.iota(jnp.int32, NEW_TOKEN_COUNT)
    new_visible = token_rows[None, :] <= token_rows[:, None]
    new_scores = jnp.where(new_visible, new_scores, -1e30)
    peak = jnp.maximum(old_scores.max(-1), new_scores.max(-1))[..., None]
    old_exp = jnp.exp(old_scores - peak)
    new_exp = jnp.exp(new_scores - peak)
    denominator = old_exp.sum(-1, keepdims=True) + new_exp.sum(-1, keepdims=True)
    old_weights = (old_exp / denominator).astype(jnp.bfloat16)
    new_weights = (new_exp / denominator).astype(jnp.bfloat16)
    mixed = jnp.einsum(
        "ckgtp,cpkd->ctkgd", old_weights, cache_values, preferred_element_type=jnp.float32
    )
    mixed = mixed + jnp.einsum(
        "ckgtu,cukd->ctkgd", new_weights, fresh_values, preferred_element_type=jnp.float32
    )
    attn_rows = mixed.reshape(
        count * NEW_TOKEN_COUNT, kv_heads * attention_clusters * ATTN_DIM
    ).astype(jnp.bfloat16)
    partial_value = jnp.dot(attn_rows, out_weight, preferred_element_type=jnp.float32)
    reward_out = lax.psum_scatter(partial_value, "tp", scatter_dimension=1, tiled=True).astype(
        jnp.bfloat16
    )
    slot_count = policy_query.shape[0]
    spread = lax.all_to_all(policy_cache, "cand", split_axis=2, concat_axis=0, tiled=True)
    selected = jnp.take(spread, source, axis=0)
    moved = lax.all_to_all(selected, "cand", split_axis=0, concat_axis=2, tiled=True)
    local_source = lax.dynamic_slice_in_dim(source, lax.axis_index("cand") * slot_count, slot_count)
    slot_lengths = jnp.take(policy_length, local_source)
    compacted = jnp.where(
        cache_rows[None, None, :, None] == slot_lengths[:, None, None, None],
        policy_new[:, :, None, :],
        moved,
    )
    slot_heads = policy_query.reshape(slot_count, kv_heads, attention_clusters, ATTN_DIM)
    slot_keys = compacted[:, 0].reshape(slot_count, CACHE_LENGTH, kv_heads, ATTN_DIM)
    slot_values = compacted[:, 1].reshape(slot_count, CACHE_LENGTH, kv_heads, ATTN_DIM)
    slot_scores = (
        jnp.einsum("skgd,spkd->skgp", slot_heads, slot_keys, preferred_element_type=jnp.float32)
        * score_scale
    )
    slot_visible = cache_rows[None, :] <= slot_lengths[:, None]
    slot_scores = jnp.where(slot_visible[:, None, None, :], slot_scores, -1e30)
    slot_weights = jax.nn.softmax(slot_scores, axis=-1).astype(jnp.bfloat16)
    policy_attn = jnp.einsum(
        "skgp,spkd->skgd", slot_weights, slot_values, preferred_element_type=jnp.float32
    )
    policy_attn = policy_attn.reshape(slot_count, kv_heads * attention_clusters * ATTN_DIM).astype(
        jnp.bfloat16
    )
    return (reward_out, compacted, policy_attn)


def solution(mesh):
    in_specs = (
        P("cand", None, "tp"),
        P("cand", None, None, "tp"),
        P("cand", None, None, "tp"),
        P("cand"),
        P("tp", None),
        P("cand", None, None, "tp"),
        P(),
        P(),
        P("cand", "tp"),
        P("cand", None, "tp"),
    )
    out_specs = (P("cand", "tp"), P("cand", None, None, "tp"), P("cand", "tp"))
    return jax.shard_map(body, mesh=mesh, in_specs=in_specs, out_specs=out_specs, check_vma=False)
```

profile of v0, /device:TPU:32, one launch (start us, length us, event | category | flops | bytes accessed | tf_op | source)
XLA Modules:
  0.0 163.1 jit_solution(17396222381493303545)
XLA Ops:
  7.2 0.0 copy-start
  7.2 5.7 %copy.68 = bf16[8,2,768,128]{3,0,1,2:T(8,128)(2,1)} copy(bf16[8,2,768,128]{3,2,1,0:T(8,128)(2,1)} %param.15) | data formatting | bytes 6291456 | tf_op args[5]
  12.9 11.5 %all-to-all-start = ((bf16[8,2,768,128]{3,0,1,2:T(8,128)(2,1)}), bf16[8,2,768,128]{3,0,1,2:T(8,128)(2,1)}, u32[]{:S(2)}, u32[]{:S(2)}) async-start(bf16[8,2,768,128]{3,0,1,2:T(8,128)(2,1)} %copy.68), calls=%async_computation.1 | async-start | bytes 6291456 | tf_op jit(solution)/shard_map/all_to_all | solution.py:68
  24.4 0.0 reduce-scatter.2.cloned.1.call-start
  24.5 0.0 copy-done.5
  24.5 0.1 iota_compare_fusion
  24.6 0.0 copy-done
  24.6 2.6 %bitcast_reduce_fusion = (f32[8,8,32]{2,1,0:T(8,128)S(1)}, f32[8,768,32,8]{1,2,3,0:T(8,128)S(1)}) fusion(pred[8,768]{1,0:T(8,128)(4,1)S(1)} %iota_compare_fusion, bf16[8,2,768,128]{3,2,1,0:T(8,128)(2,1)} %param.12, bf16[8,32,1024]{2,1,0:T(8,128)(2,1)S(1)} %copy-done), kind=kOutput, calls=%fused_computation.4 | convolution fusion | flops 407369728 | bytes 8402944 | tf_op jit(solution)/shard_map/ctkgd,cpkd->ckgtp/dot_general | solution.py:35
  27.2 0.0 copy-done.2
  27.2 0.9 fusion.39
  28.1 0.0 copy-start.6
  28.1 1.8 %fusion.2 = f32[8,8,32]{2,1,0:T(8,128)S(1)} fusion(f32[8,768,32,8]{1,2,3,0:T(8,128)S(1)} %get-tuple-element.21, f32[8,8,32]{2,1,0:T(8,128)S(1)} %max.11, pred[8,768]{1,0:T(8,128)(4,1)S(1)} %iota_compare_fusion), kind=kLoop, calls=%fused_computation.8 | loop fusion | flops 6289408 | bytes 6313984 | tf_op jit(solution)/shard_map/reduce_sum | solution.py:51
  29.9 0.0 slice-start
  29.9 0.3 fusion.20
  30.2 0.0 copy-done.6
  30.2 0.0 slice-start.1
  30.2 2.4 %fusion.3 = f32[8,8,32,128]{3,2,1,0:T(8,128)S(1)} fusion(f32[8,768,32,8]{1,2,3,0:T(8,128)S(1)} %get-tuple-element.21, f32[8,8,32]{2,1,0:T(8,128)S(1)} %add.31, f32[8,8,32]{2,1,0:T(8,128)S(1)} %max.11, pred[8,768]{1,0:T(8,128)(4,1)S(1)} %iota_compare_fusion, bf16[8,2,768,128]{3,2,1,0:T(8,128)(2,1)S(1)} %copy-done.6), kind=kOutput, calls=%fused_computation.9 | convolution fusion | flops 410517504 | bytes 8984576 | tf_op jit(solution)/shard_map/ckgtp,cpkd->ctkgd/dot_general | solution.py:54
  32.7 0.4 fusion.14
  33.1 0.2 copy.66
  33.3 0.0 slice-done
  33.3 0.1 slice-done.1
  33.4 4.3 %fusion.21 = f32[256,4096]{1,0:T(8,128)} fusion(bf16[1024,4096]{1,0:T(8,128)(2,1)S(1)} %bitcast.135, bf16[32,8,8,128]{3,2,1,0:T(8,128)(2,1)S(1)} %bitcast.138), kind=kOutput, calls=%fused_computation.37 | convolution fusion | flops 2147483648 | bytes 13107200 | tf_op jit(solution)/shard_map/dot_general | solution.py:63
  37.7 0.0 reduce-scatter.2.cloned.1.call-update
  37.7 0.6 copy-done.4
  38.4 57.1 %all-to-all-done = bf16[8,2,768,128]{3,0,1,2:T(8,128)(2,1)} async-done(((bf16[8,2,768,128]{3,0,1,2:T(8,128)(2,1)}), bf16[8,2,768,128]{3,0,1,2:T(8,128)(2,1)}, u32[]{:S(2)}, u32[]{:S(2)}) %all-to-all-start) | async-done | bytes 3145760 | tf_op jit(solution)/shard_map/all_to_all | solution.py:68
  95.5 4.4 %copy.70 = bf16[32,8,2,24,128]{4,3,2,1,0:T(8,128)(2,1)} copy(bf16[32,8,2,24,128]{4,1,2,3,0:T(8,128)(2,1)} %bitcast.23) | data formatting | bytes 6291456 | tf_op jit(solution)/shard_map/all_to_all | solution.py:68
  99.9 2.8 %gather_fusion.1 = bf16[128,2,24,128]{3,2,1,0:T(8,128)(2,1)S(1)} fusion(bf16[256,2,24,128]{3,2,1,0:T(8,128)(2,1)} %bitcast.136, s32[1024]{0:T(1024)S(1)} %pad_clamp_fusion), kind=kCustom, calls=%fused_computation.1 | custom fusion | bytes 3146240 | tf_op jit(solution)/shard_map/jit(_take)/gather | solution.py:69
  102.6 0.0 copy-start.3
  102.6 0.0 copy-start.1
  102.6 1.4 broadcast_select_fusion
  104.0 9.5 %all-to-all-start.1 = ((bf16[128,2,24,128]{3,2,1,0:T(8,128)(2,1)}), bf16[128,2,24,128]{3,2,1,0:T(8,128)(2,1)S(1)}, u32[]{:S(2)}, u32[]{:S(2)}) async-start(bf16[128,2,24,128]{3,2,1,0:T(8,128)(2,1)} %broadcast_select_fusion), calls=%async_computation.2 | async-start | bytes 3145728 | tf_op jit(solution)/shard_map/all_to_all | solution.py:70
  113.5 0.0 copy-done.3
  113.5 0.1 compare_select_fusion.1
  113.6 0.0 copy-done.1
  113.6 0.6 gather_fusion
  114.2 0.1 and_select_fusion
  114.3 0.1 iota_compare_fusion.2
  114.4 0.0 reduce-scatter.2.cloned.1.call-done
  114.4 1.8 %convert_element_type.41 = bf16[256,512]{1,0:T(8,128)(2,1)} convert(f32[256,512]{1,0:T(8,128)} %reduce-scatter.2.cloned.1.call-done) | non-fusion elementwise | flops 131072 | bytes 786432 | tf_op jit(solution)/shard_map/convert_element_type | solution.py:64
  116.2 36.5 %all-to-all-done.1 = bf16[128,2,24,128]{3,2,1,0:T(8,128)(2,1)S(1)} async-done(((bf16[128,2,24,128]{3,2,1,0:T(8,128)(2,1)}), bf16[128,2,24,128]{3,2,1,0:T(8,128)(2,1)S(1)}, u32[]{:S(2)}, u32[]{:S(2)}) %all-to-all-start.1) | async-done | bytes 1572896 | tf_op jit(solution)/shard_map/all_to_all | solution.py:70
  152.6 0.3 copy.71
  152.9 0.0 copy-start.7
  152.9 0.7 bitcast_select_fusion.1
  153.7 1.3 copy.72
  154.9 0.0 copy-done.7
  154.9 0.5 fusion.40
  155.4 0.3 fusion.19
  155.7 0.6 copy.110
  (12 shorter events, 0.1 us)
Async XLA Ops:
  7.2 17.4 %copy-start = (bf16[8,32,1024]{2,1,0:T(8,128)(2,1)S(1)}, bf16[8,32,1024]{2,1,0:T(8,128)(2,1)}, u32[]{:S(2)}) copy-start(bf16[8,32,1024]{2,1,0:T(8,128)(2,1)} %param.10) | copy-start | bytes 1572868
  12.9 11.6 %copy-start.5 = (s32[8]{0:T(128)S(1)}, s32[8]{0:T(128)}, u32[]{:S(2)}) copy-start(s32[8]{0:T(128)} %param.13) | copy-start | bytes 100
  12.9 82.6 %all-to-all-start = ((bf16[8,2,768,128]{3,0,1,2:T(8,128)(2,1)}), bf16[8,2,768,128]{3,0,1,2:T(8,128)(2,1)}, u32[]{:S(2)}, u32[]{:S(2)}) async-start(bf16[8,2,768,128]{3,0,1,2:T(8,128)(2,1)} %copy.68), calls=%async_computation.1 | async-start | bytes 6291456 | tf_op jit(solution)/shard_map/all_to_all | solution.py:68
  24.4 90.0 %reduce-scatter.2.cloned.1.call-start = ((), (), s32[]{:S(2)}) async-start(), calls=%async_computation.3 | async-start | bytes 4718592 | tf_op jit(solution)/shard_map/reduce_scatter | solution.py:64
  24.6 2.6 %copy-start.2 = (bf16[8,2,32,128]{3,2,1,0:T(8,128)(2,1)S(1)}, bf16[8,2,32,128]{3,2,1,0:T(8,128)(2,1)}, u32[]{:S(2)}) copy-start(bf16[8,2,32,128]{3,2,1,0:T(8,128)(2,1)} %param.11) | copy-start | bytes 393220
  28.1 2.1 %copy-start.6 = (bf16[8,2,768,128]{3,2,1,0:T(8,128)(2,1)S(1)}, bf16[8,2,768,128]{3,2,1,0:T(8,128)(2,1)}, u32[]{:S(2)}) copy-start(bf16[8,2,768,128]{3,2,1,0:T(8,128)(2,1)} %param.12) | copy-start | bytes 9437188
  29.9 3.4 %slice-start = ((s8[8388608]{0:T(1024)(128)(4,1)}), s8[4194304]{0:T(1024)(128)(4,1)S(1)}, s32[]{:S(2)}) async-start(s8[8388608]{0:T(1024)(128)(4,1)} %bitcast.134), calls=%async_computation.4 | async-start | bytes 8388608
  30.2 3.1 %slice-start.1 = ((s8[8388608]{0:T(1024)(128)(4,1)}), s8[4194304]{0:T(1024)(128)(4,1)S(1)}, s32[]{:S(2)}) async-start(s8[8388608]{0:T(1024)(128)(4,1)} %bitcast.134), calls=%async_computation.5 | async-start | bytes 8388608
  37.7 0.7 copy-start.4
  102.6 10.9 %copy-start.3 = (bf16[4,2,128]{2,1,0:T(2,128)(2,1)S(1)}, bf16[4,2,128]{2,1,0:T(2,128)(2,1)}, u32[]{:S(2)}) copy-start(bf16[4,2,128]{2,1,0:T(2,128)(2,1)} %param.19) | copy-start | bytes 6148
  102.6 11.0 %copy-start.1 = (s32[256]{0:T(256)S(1)}, s32[256]{0:T(256)}, u32[]{:S(2)}) copy-start(s32[256]{0:T(256)} %param.16) | copy-start | bytes 3076
  104.0 48.6 %all-to-all-start.1 = ((bf16[128,2,24,128]{3,2,1,0:T(8,128)(2,1)}), bf16[128,2,24,128]{3,2,1,0:T(8,128)(2,1)S(1)}, u32[]{:S(2)}, u32[]{:S(2)}) async-start(bf16[128,2,24,128]{3,2,1,0:T(8,128)(2,1)} %broadcast_select_fusion), calls=%async_computation.2 | async-start | bytes 3145728 | tf_op jit(solution)/shard_map/all_to_all | solution.py:70
  152.9 2.0 %copy-start.7 = (bf16[4,1024]{1,0:T(4,128)(2,1)S(1)}, bf16[4,1024]{1,0:T(4,128)(2,1)}, u32[]{:S(2)}) copy-start(bf16[4,1024]{1,0:T(4,128)(2,1)} %param.18) | copy-start | bytes 24580
Sparse Core Ops, SparseCore 0:
  37.8 42.3 reduce-scatter.1
where the time goes:
time: 164 us; the launch traced here: 163 us
  waiting for transfers between devices  93.6 us (57%)
  starting transfers between devices  21 us (13%)
  local copies, waits for them, and re-layouts  16.6 us (10%)
  between operations  14.3 us (9%)
  matrix products  11.4 us (7%)
  other arithmetic  6.26 us (4%)
    all_to_all x1, waiting for transfers between devices, body(): lax.all_to_all(policy_cache, 'cand', split_axis=2, concat_axis=0, tiled=T...  57.1 us
    all_to_all x1, waiting for transfers between devices, body(): lax.all_to_all(selected, 'cand', split_axis=0, concat_axis=2, tiled=True)  36.5 us
    all_to_all x1, starting transfers between devices, body(): lax.all_to_all(policy_cache, 'cand', split_axis=2, concat_axis=0, tiled=T...  11.5 us
    all_to_all x1, starting transfers between devices, body(): lax.all_to_all(selected, 'cand', split_axis=0, concat_axis=2, tiled=True)  9.45 us
    unnamed x24, local copies, waits for them, and re-layouts  8.31 us
    all_to_all x1, local copies, waits for them, and re-layouts, body(): lax.all_to_all(policy_cache, 'cand', split_axis=2, concat_axis=0, tiled=T...  4.41 us
    dot_general x1, matrix products, body(): jnp.dot(attn_rows, out_weight, preferred_element_type=jnp.float32)  4.33 us
  transfers between devices with their start and end apart: 3, of which 2 were waited for; matrix products, arithmetic and copies ran while one was open for 15% of the time, Pallas kernels for 0%

commit v1 on v0

--- a/solution.py
+++ b/solution.py
@@ -61,14 +61,31 @@
         count * NEW_TOKEN_COUNT, kv_heads * attention_clusters * ATTN_DIM
     ).astype(jnp.bfloat16)
     partial_value = jnp.dot(attn_rows, out_weight, preferred_element_type=jnp.float32)
-    reward_out = lax.psum_scatter(partial_value, "tp", scatter_dimension=1, tiled=True).astype(
-        jnp.bfloat16
+    pieces = partial_value.astype(jnp.bfloat16).reshape(count * NEW_TOKEN_COUNT, 8, -1)
+    pieces = lax.all_to_all(
+        pieces.transpose(1, 0, 2), "tp", split_axis=0, concat_axis=0, tiled=True
     )
+    reward_out = pieces.astype(jnp.float32).sum(0).astype(jnp.bfloat16)
     slot_count = policy_query.shape[0]
-    spread = lax.all_to_all(policy_cache, "cand", split_axis=2, concat_axis=0, tiled=True)
-    selected = jnp.take(spread, source, axis=0)
-    moved = lax.all_to_all(selected, "cand", split_axis=0, concat_axis=2, tiled=True)
-    local_source = lax.dynamic_slice_in_dim(source, lax.axis_index("cand") * slot_count, slot_count)
+    groups = source.shape[0] // slot_count
+    me = lax.axis_index("cand")
+    owner = source // count
+    same = owner[:, None] == owner[None, :]
+    slots = lax.iota(jnp.int32, source.shape[0])
+    rank = jnp.sum(same & (slots[None, :] < slots[:, None]), axis=1)
+    mine = (owner == me)[None, :] & (rank[None, :] == lax.iota(jnp.int32, slot_count)[:, None])
+    picked = jnp.sum(jnp.where(mine, (source % count)[None, :], 0), axis=1)
+    total_rows = 2 * CACHE_LENGTH
+    chunk = total_rows // groups
+    leaving = jnp.take(policy_cache.reshape(count, groups, chunk, ATTN_DIM), picked, axis=0)
+    leaving = leaving.transpose(1, 0, 2, 3)
+    spread = lax.all_to_all(leaving, "cand", split_axis=0, concat_axis=0, tiled=True)
+    spread = spread.reshape(groups * slot_count, chunk, ATTN_DIM)
+    selected = jnp.take(spread, owner * slot_count + rank, axis=0)
+    selected = selected.reshape(groups, slot_count, chunk, ATTN_DIM)
+    moved = lax.all_to_all(selected, "cand", split_axis=0, concat_axis=0, tiled=True)
+    moved = moved.transpose(1, 0, 2, 3).reshape(slot_count, 2, CACHE_LENGTH, ATTN_DIM)
+    local_source = lax.dynamic_slice_in_dim(source, me * slot_count, slot_count)
     slot_lengths = jnp.take(policy_length, local_source)
     compacted = jnp.where(
         cache_rows[None, None, :, None] == slot_lengths[:, None, None, None],

time: 164 us -> 144 us (0.88)
  between operations: 14.3 us -> 0.94 us
  waiting for transfers between devices: 93.6 us -> 83 us
  other arithmetic: 6.26 us -> 12 us
  local copies, waits for them, and re-layouts: 16.6 us -> 13.6 us
    all_to_all x2 -> x3, waiting for transfers between devices: 93.5 us -> 83 us  [the longest x1 35.6 us: body(): lax.all_to_all(selected, 'cand', split_axis=0, concat_axis=0, tiled=True)]
    unnamed x24 -> x27, local copies, waits for them, and re-layouts: 8.31 us -> 3.07 us
    select_n x2 -> x4, other arithmetic: 1.37 us -> 5.21 us  [the longest x1 2.77 us: body(): selected = jnp.take(spread, owner * slot_count + rank, axis=0)]
    all_to_all x2 -> x1, local copies, waits for them, and re-layouts: 4.69 us -> 1.51 us  [body(): lax.all_to_all(selected, 'cand', split_axis=0, concat_axis=0, tiled=True)]
    reduce_sum x0 -> x3, other arithmetic: none -> 2.95 us  [the longest x1 2.66 us: body(): reward_out = pieces.astype(jnp.float32).sum(0).astype(jnp.bfloat16)]
    gather x1 -> x2, local copies, waits for them, and re-layouts: 2.75 us -> 5.19 us  [the longest x1 3.3 us: body(): selected = jnp.take(spread, owner * slot_count + rank, axis=0)]
    dot_general x1, matrix products: 4.33 us -> 2.34 us  [body(): jnp.dot(attn_rows, out_weight, preferred_element_type=jnp.float32)]
    convert_element_type x1 -> x0, other arithmetic: 1.78 us -> none  [body(): lax.psum_scatter(partial_value, 'tp', scatter_dimension=1, tiled=True)]
  transfers between devices with their start and end apart: 3 -> 3, of which waited for: 2 -> 3; matrix products, arithmetic and copies ran while one was open for 15% -> 16% of each run, Pallas kernels for 0% -> 0%
where the time goes in v1:
time: 144 us; the launch traced here: 143 us
  waiting for transfers between devices  83 us (58%)
  starting transfers between devices  21.8 us (15%)
  local copies, waits for them, and re-layouts  13.6 us (9%)
  other arithmetic  12 us (8%)
  matrix products  11.8 us (8%)
    all_to_all x1, waiting for transfers between devices, body(): lax.all_to_all(selected, 'cand', split_axis=0, concat_axis=0, tiled=True)  35.6 us
    all_to_all x1, waiting for transfers between devices, body(): lax.all_to_all(leaving, 'cand', split_axis=0, concat_axis=0, tiled=True)  26.3 us
    all_to_all x1, waiting for transfers between devices, body(): lax.all_to_all(pieces.transpose(1, 0, 2), 'tp', split_axis=0, concat_axis...  21 us
    all_to_all x1, starting transfers between devices, body(): lax.all_to_all(leaving, 'cand', split_axis=0, concat_axis=0, tiled=True)  11.5 us
    all_to_all x1, starting transfers between devices, body(): lax.all_to_all(selected, 'cand', split_axis=0, concat_axis=0, tiled=True)  5.88 us
    all_to_all x1, starting transfers between devices, body(): lax.all_to_all(pieces.transpose(1, 0, 2), 'tp', split_axis=0, concat_axis...  4.34 us
    gather x1, local copies, waits for them, and re-layouts, body(): selected = jnp.take(spread, owner * slot_count + rank, axis=0)  3.3 us
    unnamed x27, local copies, waits for them, and re-layouts  3.07 us
  transfers between devices with their start and end apart: 3, of which 3 were waited for; matrix products, arithmetic and copies ran while one was open for 16% of the time, Pallas kernels for 0%

profile of v1, /device:TPU:32, one launch (start us, length us, event | category | flops | bytes accessed | tf_op | source)
XLA Modules:
  0.0 143.0 jit_solution(12236287127174260280)
XLA Ops:
  0.6 0.0 copy-start
  0.6 0.8 and_select_fusion
  1.5 0.8 broadcast_compare_fusion
  2.3 0.2 convert_reduce_fusion
  2.4 0.1 select_reduce_fusion
  2.6 0.0 copy-done
  2.6 1.9 %gather_fusion.1 = bf16[4,32,48,128]{3,2,1,0:T(8,128)(2,1)} fusion(bf16[8,32,48,128]{3,2,1,0:T(8,128)(2,1)S(1)} %bitcast.144, s32[1024]{0:T(1024)S(1)} %pad_clamp_fusion.1), kind=kCustom, calls=%fused_computation.1 | custom fusion | bytes 3145744 | tf_op jit(solution)/shard_map/jit(_take)/gather | solution.py:80
  4.5 1.6 %select_bitcast_fusion = bf16[32,4,48,128]{3,2,0,1:T(8,128)(2,1)S(1)} fusion(bf16[4,32,48,128]{3,2,1,0:T(8,128)(2,1)} %gather_fusion.1, pred[4]{0:T(512)(128)(4,1)S(1)} %compare_and_fusion), kind=kLoop, calls=%fused_computation.19 | loop fusion | flops 786432 | bytes 3145732 | tf_op jit(solution)/shard_map/jit(_take)/select_n | solution.py:80
  6.1 1.3 copy.73
  7.5 11.5 %all-to-all-start.1 = ((bf16[32,4,48,128]{3,2,1,0:T(8,128)(2,1)}), bf16[32,4,48,128]{3,2,1,0:T(8,128)(2,1)}, u32[]{:S(2)}, u32[]{:S(2)}) async-start(bf16[32,4,48,128]{3,2,1,0:T(8,128)(2,1)} %copy.73), calls=%async_computation.1 | async-start | bytes 3145728 | tf_op jit(solution)/shard_map/all_to_all | solution.py:82
  19.0 0.0 copy-done.7
  19.0 0.1 iota_compare_fusion.1
  19.1 2.7 %bitcast_reduce_fusion = (f32[8,8,32]{2,1,0:T(8,128)S(1)}, f32[8,768,32,8]{1,2,3,0:T(8,128)S(1)}) fusion(pred[8,768]{1,0:T(8,128)(4,1)S(1)} %iota_compare_fusion.1, bf16[8,2,768,128]{3,2,1,0:T(8,128)(2,1)} %param.12, bf16[8,32,1024]{2,1,0:T(8,128)(2,1)} %param.10), kind=kOutput, calls=%fused_computation.5 | convolution fusion | flops 407369728 | bytes 8402944 | tf_op jit(solution)/shard_map/ctkgd,cpkd->ckgtp/dot_general | solution.py:35
  21.9 0.0 copy-done.3
  21.9 0.0 copy-done.4
  21.9 0.9 fusion.41
  22.8 0.0 copy-start.8
  22.8 0.3 fusion.20
  23.1 0.0 slice-start
  23.1 1.8 %fusion.2 = f32[8,8,32]{2,1,0:T(8,128)S(1)} fusion(f32[8,768,32,8]{1,2,3,0:T(8,128)S(1)} %get-tuple-element.25, f32[8,8,32]{2,1,0:T(8,128)S(1)} %max.11, pred[8,768]{1,0:T(8,128)(4,1)S(1)} %iota_compare_fusion.1), kind=kLoop, calls=%fused_computation.10 | loop fusion | flops 6289408 | bytes 6313984 | tf_op jit(solution)/shard_map/reduce_sum | solution.py:51
  24.9 0.0 slice-start.1
  24.9 2.4 %fusion.3 = f32[8,8,32,128]{3,2,1,0:T(8,128)S(1)} fusion(f32[8,768,32,8]{1,2,3,0:T(8,128)S(1)} %get-tuple-element.25, f32[8,8,32]{2,1,0:T(8,128)S(1)} %add.54, f32[8,8,32]{2,1,0:T(8,128)S(1)} %max.11, pred[8,768]{1,0:T(8,128)(4,1)S(1)} %iota_compare_fusion.1, bf16[8,2,768,128]{3,2,1,0:T(8,128)(2,1)S(1)} %copy-done.8), kind=kOutput, calls=%fused_computation.11 | convolution fusion | flops 410517504 | bytes 8984576 | tf_op jit(solution)/shard_map/ckgtp,cpkd->ctkgd/dot_general | solution.py:54
  27.4 0.4 fusion.14
  27.8 0.2 copy.70
  28.0 2.3 %convolution_convert_fusion = bf16[256,4096]{1,0:T(8,128)(2,1)S(1)} fusion(bf16[1024,4096]{1,0:T(8,128)(2,1)S(1)} %bitcast.152, bf16[32,8,8,128]{3,2,1,0:T(8,128)(2,1)S(1)} %bitcast.149), kind=kOutput, calls=%fused_computation.9 | convolution fusion | flops 2148532224 | bytes 11010048 | tf_op jit(solution)/shard_map/dot_general | solution.py:63
  30.4 1.5 %copy.116 = bf16[32,8,8,512]{3,2,0,1:T(8,128)(2,1)} copy(bf16[32,8,8,512]{3,2,1,0:T(8,128)(2,1)S(1)} %bitcast.148) | data formatting | bytes 4194304 | tf_op jit(solution)/shard_map/reshape | solution.py:64
  31.8 26.3 %all-to-all-done.1 = bf16[32,4,48,128]{3,2,1,0:T(8,128)(2,1)} async-done(((bf16[32,4,48,128]{3,2,1,0:T(8,128)(2,1)}), bf16[32,4,48,128]{3,2,1,0:T(8,128)(2,1)}, u32[]{:S(2)}, u32[]{:S(2)}) %all-to-all-start.1) | async-done | bytes 1572896 | tf_op jit(solution)/shard_map/all_to_all | solution.py:82
  58.2 4.3 %all-to-all-start = ((bf16[8,256,512]{2,1,0:T(8,128)(2,1)}), bf16[8,256,512]{2,1,0:T(8,128)(2,1)}, u32[]{:S(2)}, u32[]{:S(2)}) async-start(bf16[8,256,512]{2,1,0:T(8,128)(2,1)} %bitcast.145), calls=%async_computation | async-start | bytes 4194304 | tf_op jit(solution)/shard_map/all_to_all | solution.py:65
  62.5 0.1 broadcast_in_dim.119
  62.7 3.3 %gather_fusion.2 = bf16[128,48,128]{2,1,0:T(8,128)(2,1)} fusion(bf16[128,48,128]{2,1,0:T(8,128)(2,1)} %bitcast.26, s32[1024]{0:T(1024)S(1)} %pad_clamp_fusion), kind=kCustom, calls=%fused_computation.2 | custom fusion | bytes 3146240 | tf_op jit(solution)/shard_map/jit(_take)/gather | solution.py:84
  66.0 2.8 %broadcast_select_fusion = bf16[32,4,48,128]{3,2,1,0:T(8,128)(2,1)} fusion(bf16[32,4,48,128]{3,2,1,0:T(8,128)(2,1)} %bitcast.147, pred[32,4]{1,0:T(8,128)(4,1)S(1)} %broadcast_in_dim.119), kind=kLoop, calls=%fused_computation.22 | loop fusion | flops 786432 | bytes 3145856 | tf_op jit(solution)/shard_map/jit(_take)/select_n | solution.py:84
  68.8 21.0 %all-to-all-done = bf16[8,256,512]{2,1,0:T(8,128)(2,1)} async-done(((bf16[8,256,512]{2,1,0:T(8,128)(2,1)}), bf16[8,256,512]{2,1,0:T(8,128)(2,1)}, u32[]{:S(2)}, u32[]{:S(2)}) %all-to-all-start) | async-done | bytes 2097184 | tf_op jit(solution)/shard_map/all_to_all | solution.py:65
  89.8 5.9 %all-to-all-start.2 = ((bf16[32,4,48,128]{3,2,1,0:T(8,128)(2,1)}), bf16[32,4,48,128]{3,2,1,0:T(8,128)(2,1)}, u32[]{:S(2)}, u32[]{:S(2)}) async-start(bf16[32,4,48,128]{3,2,1,0:T(8,128)(2,1)} %broadcast_select_fusion), calls=%async_computation.2 | async-start | bytes 3145728 | tf_op jit(solution)/shard_map/all_to_all | solution.py:86
  95.7 0.1 compare_select_fusion.3
  95.8 0.0 copy-done.1
  95.8 0.6 gather_fusion
  96.4 0.1 and_select_fusion.2
  96.5 0.1 iota_compare_fusion.3
  96.6 2.7 %reduce_sum.61 = bf16[256,512]{1,0:T(8,128)(2,1)} reduce(bf16[8,256,512]{2,1,0:T(8,128)(2,1)} %all-to-all-done, bf16[]{:T(256)} %constant.78.clone.1), dimensions={0}, to_apply=%region_4.5 | reduce | flops 917504 | bytes 2359298 | tf_op jit(solution)/shard_map/reduce_sum | solution.py:68
  99.3 35.6 %all-to-all-done.2 = bf16[32,4,48,128]{3,2,1,0:T(8,128)(2,1)} async-done(((bf16[32,4,48,128]{3,2,1,0:T(8,128)(2,1)}), bf16[32,4,48,128]{3,2,1,0:T(8,128)(2,1)}, u32[]{:S(2)}, u32[]{:S(2)}) %all-to-all-start.2) | async-done | bytes 1572896 | tf_op jit(solution)/shard_map/all_to_all | solution.py:86
  134.9 1.5 %copy.74 = bf16[32,4,48,128]{3,2,0,1:T(8,128)(2,1)S(1)} copy(bf16[32,4,48,128]{3,2,1,0:T(8,128)(2,1)} %all-to-all-done.2) | data formatting | bytes 3145728 | tf_op jit(solution)/shard_map/all_to_all | solution.py:86
  136.4 0.6 copy_select_fusion
  137.0 1.1 copy-done.2
  138.2 1.2 copy.76
  139.4 0.0 copy-done.9
  139.4 1.6 %fusion.42 = (f32[4,8]{1,0:T(4,128)S(1)}, f32[4,8,768]{2,1,0:T(8,128)S(1)}) fusion(bf16[4,2,768,128]{3,2,0,1:T(8,128)(2,1)} %copy-done.2, pred[4,768]{1,0:T(4,128)(4,1)S(1)} %get-tuple-element.22, bf16[1,4,8,128]{3,1,2,0:T(4,128)(2,1)S(1)} %bitcast.153), kind=kOutput, calls=%fused_computation.88 | convolution fusion | flops 6390527 | bytes 896128 | tf_op jit(solution)/shard_map/sub | solution.py:104
  141.0 1.4 fusion.19
  142.4 0.6 copy.117
  (24 shorter events, 0.1 us)
Async XLA Ops:
  0.6 2.0 %copy-start = (bf16[8,2,768,128]{3,2,1,0:T(8,128)(2,1)S(1)}, bf16[8,2,768,128]{3,2,1,0:T(8,128)(2,1)}, u32[]{:S(2)}) copy-start(bf16[8,2,768,128]{3,2,1,0:T(8,128)(2,1)} %param.15) | copy-start | bytes 9437188
  7.5 11.6 %copy-start.7 = (s32[8]{0:T(128)S(1)}, s32[8]{0:T(128)}, u32[]{:S(2)}) copy-start(s32[8]{0:T(128)} %param.13) | copy-start | bytes 100
  7.5 50.7 %all-to-all-start.1 = ((bf16[32,4,48,128]{3,2,1,0:T(8,128)(2,1)}), bf16[32,4,48,128]{3,2,1,0:T(8,128)(2,1)}, u32[]{:S(2)}, u32[]{:S(2)}) async-start(bf16[32,4,48,128]{3,2,1,0:T(8,128)(2,1)} %copy.73), calls=%async_computation.1 | async-start | bytes 3145728 | tf_op jit(solution)/shard_map/all_to_all | solution.py:82
  19.1 2.8 %copy-start.3 = (bf16[8,32,1024]{2,1,0:T(8,128)(2,1)S(1)}, bf16[8,32,1024]{2,1,0:T(8,128)(2,1)}, u32[]{:S(2)}) copy-start(bf16[8,32,1024]{2,1,0:T(8,128)(2,1)} %param.10) | copy-start | bytes 1572868
  19.1 2.8 %copy-start.4 = (bf16[8,2,32,128]{3,2,1,0:T(8,128)(2,1)S(1)}, bf16[8,2,32,128]{3,2,1,0:T(8,128)(2,1)}, u32[]{:S(2)}) copy-start(bf16[8,2,32,128]{3,2,1,0:T(8,128)(2,1)} %param.11) | copy-start | bytes 393220
  22.8 2.1 %copy-start.8 = (bf16[8,2,768,128]{3,2,1,0:T(8,128)(2,1)S(1)}, bf16[8,2,768,128]{3,2,1,0:T(8,128)(2,1)}, u32[]{:S(2)}) copy-start(bf16[8,2,768,128]{3,2,1,0:T(8,128)(2,1)} %param.12) | copy-start | bytes 9437188
  23.1 4.9 %slice-start = ((s8[8388608]{0:T(1024)(128)(4,1)}), s8[4194304]{0:T(1024)(128)(4,1)S(1)}, s32[]{:S(2)}) async-start(s8[8388608]{0:T(1024)(128)(4,1)} %bitcast.151), calls=%async_computation.3 | async-start | bytes 8388608
  24.9 3.1 %slice-start.1 = ((s8[8388608]{0:T(1024)(128)(4,1)}), s8[4194304]{0:T(1024)(128)(4,1)S(1)}, s32[]{:S(2)}) async-start(s8[8388608]{0:T(1024)(128)(4,1)} %bitcast.151), calls=%async_computation.4 | async-start | bytes 8388608
  58.2 31.6 %all-to-all-start = ((bf16[8,256,512]{2,1,0:T(8,128)(2,1)}), bf16[8,256,512]{2,1,0:T(8,128)(2,1)}, u32[]{:S(2)}, u32[]{:S(2)}) async-start(bf16[8,256,512]{2,1,0:T(8,128)(2,1)} %bitcast.145), calls=%async_computation | async-start | bytes 4194304 | tf_op jit(solution)/shard_map/all_to_all | solution.py:65
  68.7 26.9 %copy-start.5 = (bf16[4,2,128]{2,1,0:T(2,128)(2,1)S(1)}, bf16[4,2,128]{2,1,0:T(2,128)(2,1)}, u32[]{:S(2)}) copy-start(bf16[4,2,128]{2,1,0:T(2,128)(2,1)} %param.19) | copy-start | bytes 6148
  68.7 27.0 %copy-start.6 = (s32[128]{0:T(128)S(1)}, s32[128]{0:T(128)}, u32[]{:S(2)}) copy-start(s32[128]{0:T(128)} %param.17) | copy-start | bytes 1540
  68.8 27.1 %copy-start.1 = (s32[256]{0:T(256)S(1)}, s32[256]{0:T(256)}, u32[]{:S(2)}) copy-start(s32[256]{0:T(256)} %param.16) | copy-start | bytes 3076
  89.8 45.1 %all-to-all-start.2 = ((bf16[32,4,48,128]{3,2,1,0:T(8,128)(2,1)}), bf16[32,4,48,128]{3,2,1,0:T(8,128)(2,1)}, u32[]{:S(2)}, u32[]{:S(2)}) async-start(bf16[32,4,48,128]{3,2,1,0:T(8,128)(2,1)} %broadcast_select_fusion), calls=%async_computation.2 | async-start | bytes 3145728 | tf_op jit(solution)/shard_map/all_to_all | solution.py:86
  137.0 1.2 copy-start.2
  138.2 1.2 copy-start.9

commit v2 on v0

v2 whole, which is shorter than its diff:
```python
import functools

import jax
import jax.numpy as jnp
from jax import lax
from jax.experimental import pallas as pl
from jax.experimental.pallas import tpu as pltpu
from jax.sharding import PartitionSpec as P

ASKING_UNITS = 64
SHARED_KV_UNITS = 8
ATTN_DIM = 128
NEW_TOKEN_COUNT = 32
CACHE_LENGTH = 768
PER_KV = ASKING_UNITS // SHARED_KV_UNITS
ROWS = 2 * CACHE_LENGTH
SCALE = ATTN_DIM ** (-0.5)
PARTS = 3


def score(rows, keys):
    return lax.dot_general(
        rows, keys, (((1,), (1,)), ((), ())), preferred_element_type=jnp.float32
    )


def exchange_kernel(
    groups,
    shares,
    slots,
    picked,
    chosen,
    lengths,
    query_hbm,
    new_hbm,
    kv_hbm,
    weight_hbm,
    cache_hbm,
    out_ref,
    moved_ref,
    cache,
    leaving,
    arrived0,
    arrived1,
    arrived2,
    sorted_rows,
    query,
    new,
    kv,
    weight,
    attn,
    pieces,
    others,
    load_sem,
    send1,
    recv1,
    send2,
    recv2,
    send3,
    recv3,
    own_sem,
):
    arrived = (arrived0, arrived1, arrived2)
    me = lax.axis_index("cand")
    share = lax.axis_index("tp")
    chunk = ROWS // groups
    part = chunk // PARTS
    count = query.shape[0]
    width = pieces.shape[2]

    loads = [
        pltpu.make_async_copy(cache_hbm, cache, load_sem.at[0]),
        pltpu.make_async_copy(query_hbm, query, load_sem.at[1]),
        pltpu.make_async_copy(new_hbm, new, load_sem.at[2]),
        pltpu.make_async_copy(kv_hbm, kv, load_sem.at[3]),
        pltpu.make_async_copy(weight_hbm, weight, load_sem.at[4]),
    ]
    for load in loads:
        load.start()

    barrier = pltpu.get_barrier_semaphore()

    @pl.loop(1, groups)
    def _(i):
        pl.semaphore_signal(barrier, inc=1, device_id={"cand": lax.rem(me + i, groups)})

    @pl.loop(1, shares)
    def _(i):
        pl.semaphore_signal(barrier, inc=1, device_id={"tp": lax.rem(share + i, shares)})

    loads[0].wait()
    step = 128

    @pl.loop(0, ROWS // step)
    def _(i):
        rows = pl.ds(pl.multiple_of(i * step, step), step)
        for k in range(slots):
            leaving[k, rows, :] = cache[picked[k], rows, :]

    pl.semaphore_wait(barrier, groups + shares - 2)

    def first(h, i):
        peer = lax.rem(me + i, groups)
        rows = pl.ds(pl.multiple_of(peer * chunk + h * part, part), part)
        return pltpu.make_async_remote_copy(
            src_ref=leaving.at[:, rows, :],
            dst_ref=arrived[h].at[pl.ds(i * slots, slots)],
            send_sem=send1.at[h],
            recv_sem=recv1.at[h],
            device_id={"cand": peer},
        )

    for h in range(PARTS):

        @pl.loop(1, groups)
        def _(t):
            first(h, lax.rem(t * 5, groups)).start()

        rows = pl.ds(pl.multiple_of(me * chunk + h * part, part), part)
        for k in range(slots):
            arrived[h][k] = leaving[k, rows, :]

    for load in loads[1:4]:
        load.wait()
    lead = PER_KV * NEW_TOKEN_COUNT
    tokens = lax.broadcasted_iota(jnp.int32, (lead, NEW_TOKEN_COUNT), 0) % NEW_TOKEN_COUNT
    fresh = lax.broadcasted_iota(jnp.int32, (lead, NEW_TOKEN_COUNT), 1) <= tokens
    place = lax.broadcasted_iota(jnp.int32, (lead, CACHE_LENGTH), 1)

    @pl.loop(0, count)
    def _(c):
        heads = jnp.concatenate(
            [query[c, :, g * ATTN_DIM : (g + 1) * ATTN_DIM] for g in range(PER_KV)], axis=0
        )
        old = jnp.where(place < lengths[c], score(heads, kv[c, 0]) * SCALE, -1e30)
        now = jnp.where(fresh, score(heads, new[c, 0]) * SCALE, -1e30)
        peak = jnp.maximum(old.max(-1, keepdims=True), now.max(-1, keepdims=True))
        old = jnp.exp(old - peak)
        now = jnp.exp(now - peak)
        inverse = 1.0 / (old.sum(-1, keepdims=True) + now.sum(-1, keepdims=True))
        mixed = jnp.dot(
            (old * inverse).astype(jnp.bfloat16), kv[c, 1], preferred_element_type=jnp.float32
        ) + jnp.dot(
            (now * inverse).astype(jnp.bfloat16), new[c, 1], preferred_element_type=jnp.float32
        )
        mixed = mixed.astype(jnp.bfloat16)
        rows = pl.ds(pl.multiple_of(c * NEW_TOKEN_COUNT, NEW_TOKEN_COUNT), NEW_TOKEN_COUNT)
        for g in range(PER_KV):
            attn[rows, g * ATTN_DIM : (g + 1) * ATTN_DIM] = mixed[
                g * NEW_TOKEN_COUNT : (g + 1) * NEW_TOKEN_COUNT
            ]

    loads[4].wait()

    @pl.loop(0, shares)
    def _(p):
        columns = pl.ds(pl.multiple_of(p * width, width), width)
        pieces[p] = jnp.dot(
            attn[...], weight[:, columns], preferred_element_type=jnp.float32
        ).astype(jnp.bfloat16)

    def across(i):
        peer = lax.rem(share + i, shares)
        return pltpu.make_async_remote_copy(
            src_ref=pieces.at[peer],
            dst_ref=others.at[i - 1],
            send_sem=send3,
            recv_sem=recv3,
            device_id={"tp": peer},
        )

    @pl.loop(1, shares)
    def _(i):
        across(i).start()

    def second(h, i):
        peer = lax.rem(me + i, groups)
        rows = pl.ds(pl.multiple_of(me * chunk + h * part, part), part)
        return pltpu.make_async_remote_copy(
            src_ref=sorted_rows.at[pl.ds((h * groups + peer) * slots, slots)],
            dst_ref=moved_ref.at[:, rows, :],
            send_sem=send2,
            recv_sem=recv2,
            device_id={"cand": peer},
        )

    def keep(h):
        rows = pl.ds(pl.multiple_of(me * chunk + h * part, part), part)
        return pltpu.make_async_copy(
            sorted_rows.at[pl.ds((h * groups + me) * slots, slots)],
            moved_ref.at[:, rows, :],
            own_sem.at[h],
        )

    incoming = (groups - 1) * slots
    for h in range(PARTS):
        pltpu.make_async_copy(
            arrived[h].at[pl.ds(0, incoming)], arrived[h].at[pl.ds(slots, incoming)], recv1.at[h]
        ).wait()

        @pl.loop(0, groups)
        def _(g):
            for k in range(slots):
                s = g * slots + k
                sorted_rows[h * groups * slots + s] = arrived[h][chosen[s]]

        @pl.loop(1, groups)
        def _(t):
            second(h, lax.rem(t * 5, groups)).start()

        keep(h).start()

    pltpu.make_async_copy(others, others, recv3).wait()
    block = 32

    @pl.loop(0, out_ref.shape[0] // block)
    def _(r):
        rows = pl.ds(pl.multiple_of(r * block, block), block)
        total = pieces[share, rows, :].astype(jnp.float32)
        for i in range(shares - 1):
            total = total + others[i, rows, :].astype(jnp.float32)
        out_ref[rows, :] = total.astype(jnp.bfloat16)

    pltpu.make_async_copy(others, others, send3).wait()
    for h in range(PARTS):
        pltpu.make_async_copy(
            arrived[h].at[pl.ds(0, incoming)], arrived[h].at[pl.ds(slots, incoming)], send1.at[h]
        ).wait()
        keep(h).wait()
    everything = PARTS * incoming
    for sem in (send2, recv2):
        pltpu.make_async_copy(
            sorted_rows.at[pl.ds(0, everything)], sorted_rows.at[pl.ds(0, everything)], sem
        ).wait()


def exchange(groups, shares, slots, picked, chosen, lengths, query, new, kv, weight, cache):
    count = query.shape[0]
    chunk = ROWS // groups
    part = chunk // PARTS
    bf16 = jnp.bfloat16
    width = weight.shape[1] // shares
    lead = count * NEW_TOKEN_COUNT
    smem = pl.BlockSpec(memory_space=pltpu.SMEM)
    anywhere = pl.BlockSpec(memory_space=pl.ANY)
    dma = pltpu.SemaphoreType.DMA
    return pl.pallas_call(
        functools.partial(exchange_kernel, groups, shares, slots),
        out_shape=(
            jax.ShapeDtypeStruct((lead, width), bf16),
            jax.ShapeDtypeStruct((slots, ROWS, ATTN_DIM), bf16),
        ),
        in_specs=[smem] * 3 + [anywhere] * 5,
        out_specs=(pl.BlockSpec(memory_space=pltpu.VMEM), anywhere),
        scratch_shapes=[
            pltpu.VMEM((count, ROWS, ATTN_DIM), bf16),
            pltpu.VMEM((slots, ROWS, ATTN_DIM), bf16),
            pltpu.VMEM((groups * slots, part, ATTN_DIM), bf16),
            pltpu.VMEM((groups * slots, part, ATTN_DIM), bf16),
            pltpu.VMEM((groups * slots, part, ATTN_DIM), bf16),
            pltpu.VMEM((PARTS * groups * slots, part, ATTN_DIM), bf16),
            pltpu.VMEM(query.shape, bf16),
            pltpu.VMEM(new.shape, bf16),
            pltpu.VMEM(kv.shape, bf16),
            pltpu.VMEM(weight.shape, bf16),
            pltpu.VMEM((lead, weight.shape[0]), bf16),
            pltpu.VMEM((shares, lead, width), bf16),
            pltpu.VMEM((shares - 1, lead, width), bf16),
            dma((5,)),
            dma((PARTS,)),
            dma((PARTS,)),
            dma,
            dma,
            dma,
            dma,
            dma((PARTS,)),
        ],
        compiler_params=pltpu.CompilerParams(
            collective_id=0, has_side_effects=True, vmem_limit_bytes=60 * 1024 * 1024
        ),
        name="exchange",
    )(picked, chosen, lengths, query, new, kv, weight, cache)


def policy_kernel(lengths, moved, new, query, kept, out, rows_out):
    s = pl.program_id(0)
    slots = query.shape[0]
    length = lengths[s]
    row = lax.broadcasted_iota(jnp.int32, (CACHE_LENGTH, ATTN_DIM), 0)
    keys = jnp.where(row == length, new[0, 0:1, :], moved[0, 0:CACHE_LENGTH, :])
    values = jnp.where(row == length, new[0, 1:2, :], moved[0, CACHE_LENGTH:ROWS, :])
    kept[0, 0] = keys
    kept[0, 1] = values
    which = lax.broadcasted_iota(jnp.int32, query.shape, 0)
    line = jnp.where(which == s, query[...].astype(jnp.float32), 0.0).sum(0, keepdims=True)
    heads = jnp.concatenate(
        [line[:, g * ATTN_DIM : (g + 1) * ATTN_DIM] for g in range(PER_KV)], axis=0
    ).astype(jnp.bfloat16)
    place = lax.broadcasted_iota(jnp.int32, (PER_KV, CACHE_LENGTH), 1)
    found = jnp.where(place <= length, score(heads, keys) * SCALE, -1e30)
    found = jnp.exp(found - found.max(-1, keepdims=True))
    found = found * (1.0 / found.sum(-1, keepdims=True))
    mixed = jnp.dot(found.astype(jnp.bfloat16), values, preferred_element_type=jnp.float32)
    line = jnp.concatenate([mixed[g : g + 1] for g in range(PER_KV)], axis=1)

    @pl.when(s == 0)
    def _():
        rows_out[...] = jnp.zeros_like(rows_out)

    rows_out[...] = jnp.where(which == s, line, rows_out[...])

    @pl.when(s == slots - 1)
    def _():
        out[...] = rows_out[...].astype(jnp.bfloat16)


def policy(lengths, moved, new, query):
    slots = query.shape[0]
    bf16 = jnp.bfloat16
    whole = pl.BlockSpec(query.shape, lambda s, lens: (0, 0))
    return pl.pallas_call(
        policy_kernel,
        out_shape=(
            jax.ShapeDtypeStruct((slots, 2, CACHE_LENGTH, ATTN_DIM), bf16),
            jax.ShapeDtypeStruct(query.shape, bf16),
        ),
        grid_spec=pltpu.PrefetchScalarGridSpec(
            num_scalar_prefetch=1,
            grid=(slots,),
            in_specs=[
                pl.BlockSpec((1, ROWS, ATTN_DIM), lambda s, lens: (s, 0, 0)),
                pl.BlockSpec((1, 2, ATTN_DIM), lambda s, lens: (s, 0, 0)),
                whole,
            ],
            out_specs=(
                pl.BlockSpec((1, 2, CACHE_LENGTH, ATTN_DIM), lambda s, lens: (s, 0, 0, 0)),
                whole,
            ),
            scratch_shapes=[pltpu.VMEM(query.shape, jnp.float32)],
        ),
        name="policy",
    )(lengths, moved, new, query)


def body(
    groups,
    shares,
    reward_query,
    reward_new,
    reward_key_value_cache,
    reward_length,
    out_weight,
    policy_cache,
    policy_length,
    source,
    policy_query,
    policy_new,
):
    count = reward_query.shape[0]
    slots = policy_query.shape[0]
    me = lax.axis_index("cand")
    owner = source // count
    same = owner[:, None] == owner[None, :]
    order = lax.iota(jnp.int32, source.shape[0])
    rank = jnp.sum(same & (order[None, :] < order[:, None]), axis=1)
    mine = (owner == me)[None, :] & (rank[None, :] == lax.iota(jnp.int32, slots)[:, None])
    picked = jnp.sum(jnp.where(mine, (source % count)[None, :], 0), axis=1)
    chosen = ((me - owner + groups) % groups) * slots + rank
    reward_out, moved = exchange(
        groups,
        shares,
        slots,
        picked,
        chosen,
        reward_length,
        reward_query,
        reward_new,
        reward_key_value_cache,
        out_weight,
        policy_cache.reshape(count, ROWS, ATTN_DIM),
    )
    local_source = lax.dynamic_slice_in_dim(source, me * slots, slots)
    slot_lengths = jnp.take(policy_length, local_source)
    compacted, policy_attn = policy(slot_lengths, moved, policy_new, policy_query)
    return (reward_out, compacted, policy_attn)


def solution(mesh):
    in_specs = (
        P("cand", None, "tp"),
        P("cand", None, None, "tp"),
        P("cand", None, None, "tp"),
        P("cand"),
        P("tp", None),
        P("cand", None, None, "tp"),
        P(),
        P(),
        P("cand", "tp"),
        P("cand", None, "tp"),
    )
    out_specs = (P("cand", "tp"), P("cand", None, None, "tp"), P("cand", "tp"))
    return jax.shard_map(
        functools.partial(body, mesh.shape["cand"], mesh.shape["tp"]),
        mesh=mesh,
        in_specs=in_specs,
        out_specs=out_specs,
        check_vma=False,
    )
```

time: 164 us -> 95.3 us (0.58)
  waiting for transfers between devices: 93.6 us -> 0 us
  Pallas kernels: 0 us -> 87.5 us
  starting transfers between devices: 21 us -> 0 us
  local copies, waits for them, and re-layouts: 16.6 us -> 2.32 us
  between operations: 14.3 us -> 0.66 us
  matrix products: 11.4 us -> 0 us
    all_to_all x2 -> x0, waiting for transfers between devices: 93.5 us -> none  [the longest x1 57.1 us: body(): lax.all_to_all(policy_cache, 'cand', split_axis=2, concat_axis=0, tiled=T...]
    pallas_call x0 -> x2, Pallas kernels: none -> 87.5 us  [the longest x1 82.2 us: exchange(): pl.pallas_call(functools.partial(exchange_kernel, groups, shares, slots),...]
    all_to_all x2 -> x0, starting transfers between devices: 21 us -> none  [the longest x1 11.5 us: body(): lax.all_to_all(policy_cache, 'cand', split_axis=2, concat_axis=0, tiled=T...]
    dot_general x6 -> x0, matrix products: 10.9 us -> none  [the longest x1 4.33 us: body(): jnp.dot(attn_rows, out_weight, preferred_element_type=jnp.float32)]
    unnamed x24 -> x3, local copies, waits for them, and re-layouts: 8.31 us -> 1.68 us
    all_to_all x2 -> x0, local copies, waits for them, and re-layouts: 4.69 us -> none  [the longest x1 4.41 us: body(): lax.all_to_all(policy_cache, 'cand', split_axis=2, concat_axis=0, tiled=T...]
    gather x1 -> x0, local copies, waits for them, and re-layouts: 2.75 us -> none  [body(): selected = jnp.take(spread, source, axis=0)]
    select_n x2, other arithmetic: 0.16 us -> 1.98 us  [body(): slot_lengths = jnp.take(policy_length, local_source)]
  transfers between devices with their start and end apart: 3 -> 0, of which waited for: 2 -> 0; matrix products, arithmetic and copies ran while one was open for 15% -> 0% of each run, Pallas kernels for 0% -> 0%
where the time goes in v2:
time: 95.3 us; the launch traced here: 95.1 us
  Pallas kernels  87.5 us (92%)
  other arithmetic  4.65 us (5%)
  local copies, waits for them, and re-layouts  2.32 us (2%)
    pallas_call x1, Pallas kernels, exchange(): pl.pallas_call(functools.partial(exchange_kernel, groups, shares, slots),...  82.2 us
    pallas_call x1, Pallas kernels, policy(): pl.pallas_call(policy_kernel, out_shape=(jax.ShapeDtypeStruct((slots, 2,...  5.26 us
    select_n x2, other arithmetic, body(): slot_lengths = jnp.take(policy_length, local_source)  1.98 us

profile of v2, /device:TPU:32, one launch (start us, length us, event | category | flops | bytes accessed | tf_op | source)
XLA Modules:
  0.0 95.1 jit_solution(15774923904274013780)
XLA Ops:
  0.6 0.0 copy-start
  0.6 0.7 compare_select_fusion
  1.4 0.7 and_select_fusion.2
  2.0 0.7 broadcast_compare_fusion
  2.7 0.2 convert_reduce_fusion
  2.9 0.5 fusion.3.chosen
  3.4 0.6 select_reduce_fusion.picked
  4.1 0.0 copy-done
  4.1 0.6 gather_fusion
  4.7 1.2 %and_select_fusion.lengths = s32[4]{0:T(128)} fusion(s32[4]{0:T(128)S(1)} %gather_fusion, s32[128]{0:T(128)} %param.17, s32[]{:T(128)S(6)} %select_n.36), kind=kLoop, calls=%fused_computation.11 | loop fusion | flops 28 | bytes 52 | tf_op jit(solution)/shard_map/jit(_take)/select_n | solution.py:383
  5.9 82.2 %exchange.1 = (bf16[256,512]{1,0:T(8,128)(2,1)}, bf16[4,1536,128]{2,1,0:T(8,128)(2,1)}) custom-call(s32[4]{0:T(128)} %select_reduce_fusion.picked, s32[128]{0:T(128)} %fusion.3.chosen, s32[8]{0:T(128)} %lengths.1, bf16[8,32,1024]{2,1,0:T(8,128)(2,1)} %query_hbm.1, bf16[8,2,32,128]{3,2,1,0:T(8,128)(2,1)} %new_hbm.1, bf16[8,2,768,128]{3,2,1,0:T(8,128)(2,1)} %kv_hbm.1, ...), custom_call_target="tpu_custom_call" | custom-call | tf_op jit(solution)/shard_map/exchange/pallas_call | solution.py:247
  88.2 5.3 %policy.1 = (bf16[4,2,768,128]{3,2,1,0:T(8,128)(2,1)}, bf16[4,1024]{1,0:T(4,128)(2,1)}) custom-call(s32[4]{0:T(128)} %and_select_fusion.lengths, bf16[4,1536,128]{2,1,0:T(8,128)(2,1)} %get-tuple-element.8.moved, bf16[4,2,128]{2,1,0:T(2,128)(2,1)} %new.1, bf16[4,1024]{1,0:T(4,128)(2,1)} %query.1), custom_call_target="tpu_custom_call" | custom-call | tf_op jit(solution)/shard_map/policy/pallas_call | solution.py:321
  93.4 1.7 %copy.14 = bf16[256,512]{1,0:T(8,128)(2,1)} copy(bf16[256,512]{1,0:T(8,128)(2,1)} %get-tuple-element.16) | data formatting | bytes 524288
  (1 shorter events, 0.0 us)
Async XLA Ops:
  0.6 3.4 %copy-start = (s32[256]{0:T(256)S(1)}, s32[256]{0:T(256)}, u32[]{:S(2)}) copy-start(s32[256]{0:T(256)} %param.16) | copy-start | bytes 3076

commit v3 on v2

v3 whole, which is shorter than its diff:
```python
import functools

import jax
import jax.numpy as jnp
from jax import lax
from jax.experimental import pallas as pl
from jax.experimental.pallas import tpu as pltpu
from jax.sharding import PartitionSpec as P

ASKING_UNITS = 64
SHARED_KV_UNITS = 8
ATTN_DIM = 128
NEW_TOKEN_COUNT = 32
CACHE_LENGTH = 768
PER_KV = ASKING_UNITS // SHARED_KV_UNITS
ROWS = 2 * CACHE_LENGTH
SCALE = ATTN_DIM ** (-0.5)
PARTS = 3


def score(rows, keys):
    return lax.dot_general(
        rows, keys, (((1,), (1,)), ((), ())), preferred_element_type=jnp.float32
    )


def exchange_kernel(
    groups,
    shares,
    slots,
    chosen,
    lengths,
    query_hbm,
    new_hbm,
    kv_hbm,
    weight_hbm,
    cache_hbm,
    out_ref,
    moved_ref,
    cache0,
    cache1,
    cache2,
    leaving0,
    leaving1,
    leaving2,
    arrived0,
    arrived1,
    arrived2,
    sorted_rows,
    query,
    new,
    kv,
    weight,
    attn,
    pieces,
    others,
    span_sem,
    load_sem,
    send1,
    recv1,
    send2,
    recv2,
    send3,
    recv3,
    own_sem,
):
    cache = (cache0, cache1, cache2)
    leaving = (leaving0, leaving1, leaving2)
    arrived = (arrived0, arrived1, arrived2)
    me = lax.axis_index("cand")
    share = lax.axis_index("tp")
    span = ROWS // PARTS
    part = span // groups
    count = query.shape[0]
    width = pieces.shape[2]

    spans = [
        pltpu.make_async_copy(
            cache_hbm.at[:, pl.ds(h * span, span), :], cache[h], span_sem.at[h]
        )
        for h in range(PARTS)
    ]
    loads = [
        pltpu.make_async_copy(query_hbm, query, load_sem.at[0]),
        pltpu.make_async_copy(new_hbm, new, load_sem.at[1]),
        pltpu.make_async_copy(kv_hbm, kv, load_sem.at[2]),
        pltpu.make_async_copy(weight_hbm, weight, load_sem.at[3]),
    ]
    for load in spans:
        load.start()

    barrier = pltpu.get_barrier_semaphore()

    @pl.loop(1, groups)
    def _(i):
        pl.semaphore_signal(barrier, inc=1, device_id={"cand": lax.rem(me + i, groups)})

    @pl.loop(1, shares)
    def _(i):
        pl.semaphore_signal(barrier, inc=1, device_id={"tp": lax.rem(share + i, shares)})

    step = 128

    def pick(h):
        @pl.loop(0, span // step)
        def _(i):
            rows = pl.ds(pl.multiple_of(i * step, step), step)
            for k in range(slots):
                leaving[h][k, rows, :] = cache[h][chosen[1, k], rows, :]

    def first(h, i):
        peer = lax.rem(me + i, groups)
        rows = pl.ds(pl.multiple_of(peer * part, part), part)
        return pltpu.make_async_remote_copy(
            src_ref=leaving[h].at[:, rows, :],
            dst_ref=arrived[h].at[pl.ds(i * slots, slots)],
            send_sem=send1.at[h],
            recv_sem=recv1.at[h],
            device_id={"cand": peer},
        )

    for h in range(PARTS):
        spans[h].wait()
        pick(h)
        if h == 0:
            pl.semaphore_wait(barrier, groups + shares - 2)

        @pl.loop(1, groups)
        def _(t):
            first(h, lax.rem(t * 5, groups)).start()

        rows = pl.ds(pl.multiple_of(me * part, part), part)
        for k in range(slots):
            arrived[h][k] = leaving[h][k, rows, :]

    for load in loads:
        load.start()
    for load in loads[:3]:
        load.wait()
    lead = PER_KV * NEW_TOKEN_COUNT
    tokens = lax.broadcasted_iota(jnp.int32, (lead, NEW_TOKEN_COUNT), 0) % NEW_TOKEN_COUNT
    fresh = lax.broadcasted_iota(jnp.int32, (lead, NEW_TOKEN_COUNT), 1) <= tokens
    place = lax.broadcasted_iota(jnp.int32, (lead, CACHE_LENGTH), 1)

    @pl.loop(0, count)
    def _(c):
        heads = jnp.concatenate(
            [query[c, :, g * ATTN_DIM : (g + 1) * ATTN_DIM] for g in range(PER_KV)], axis=0
        )
        old = jnp.where(place < lengths[c], score(heads, kv[c, 0]) * SCALE, -1e30)
        now = jnp.where(fresh, score(heads, new[c, 0]) * SCALE, -1e30)
        peak = jnp.maximum(old.max(-1, keepdims=True), now.max(-1, keepdims=True))
        old = jnp.exp(old - peak)
        now = jnp.exp(now - peak)
        inverse = 1.0 / (old.sum(-1, keepdims=True) + now.sum(-1, keepdims=True))
        mixed = jnp.dot(
            (old * inverse).astype(jnp.bfloat16), kv[c, 1], preferred_element_type=jnp.float32
        ) + jnp.dot(
            (now * inverse).astype(jnp.bfloat16), new[c, 1], preferred_element_type=jnp.float32
        )
        mixed = mixed.astype(jnp.bfloat16)
        rows = pl.ds(pl.multiple_of(c * NEW_TOKEN_COUNT, NEW_TOKEN_COUNT), NEW_TOKEN_COUNT)
        for g in range(PER_KV):
            attn[rows, g * ATTN_DIM : (g + 1) * ATTN_DIM] = mixed[
                g * NEW_TOKEN_COUNT : (g + 1) * NEW_TOKEN_COUNT
            ]

    loads[3].wait()

    @pl.loop(0, shares)
    def _(p):
        columns = pl.ds(pl.multiple_of(p * width, width), width)
        pieces[p] = jnp.dot(
            attn[...], weight[:, columns], preferred_element_type=jnp.float32
        ).astype(jnp.bfloat16)

    def across(i):
        peer = lax.rem(share + i, shares)
        return pltpu.make_async_remote_copy(
            src_ref=pieces.at[peer],
            dst_ref=others.at[i - 1],
            send_sem=send3,
            recv_sem=recv3,
            device_id={"tp": peer},
        )

    @pl.loop(1, shares)
    def _(i):
        across(i).start()

    def second(h, i):
        peer = lax.rem(me + i, groups)
        rows = pl.ds(pl.multiple_of(h * span + me * part, part), part)
        return pltpu.make_async_remote_copy(
            src_ref=sorted_rows.at[pl.ds((h * groups + peer) * slots, slots)],
            dst_ref=moved_ref.at[:, rows, :],
            send_sem=send2,
            recv_sem=recv2,
            device_id={"cand": peer},
        )

    def keep(h):
        rows = pl.ds(pl.multiple_of(h * span + me * part, part), part)
        return pltpu.make_async_copy(
            sorted_rows.at[pl.ds((h * groups + me) * slots, slots)],
            moved_ref.at[:, rows, :],
            own_sem.at[h],
        )

    incoming = (groups - 1) * slots
    for h in range(PARTS):
        pltpu.make_async_copy(
            arrived[h].at[pl.ds(0, incoming)], arrived[h].at[pl.ds(slots, incoming)], recv1.at[h]
        ).wait()

        @pl.loop(0, groups)
        def _(g):
            for k in range(slots):
                s = g * slots + k
                sorted_rows[h * groups * slots + s] = arrived[h][chosen[0, s]]

        @pl.loop(1, groups)
        def _(t):
            second(h, lax.rem(t * 5, groups)).start()

        keep(h).start()

    pltpu.make_async_copy(others, others, recv3).wait()
    block = 32

    @pl.loop(0, out_ref.shape[0] // block)
    def _(r):
        rows = pl.ds(pl.multiple_of(r * block, block), block)
        total = pieces[share, rows, :].astype(jnp.float32)
        for i in range(shares - 1):
            total = total + others[i, rows, :].astype(jnp.float32)
        out_ref[rows, :] = total.astype(jnp.bfloat16)

    pltpu.make_async_copy(others, others, send3).wait()
    for h in range(PARTS):
        pltpu.make_async_copy(
            arrived[h].at[pl.ds(0, incoming)], arrived[h].at[pl.ds(slots, incoming)], send1.at[h]
        ).wait()
        keep(h).wait()
    everything = PARTS * incoming
    for sem in (send2, recv2):
        pltpu.make_async_copy(
            sorted_rows.at[pl.ds(0, everything)], sorted_rows.at[pl.ds(0, everything)], sem
        ).wait()


def exchange(groups, shares, slots, chosen, lengths, query, new, kv, weight, cache):
    count = query.shape[0]
    part = ROWS // groups // PARTS
    bf16 = jnp.bfloat16
    width = weight.shape[1] // shares
    lead = count * NEW_TOKEN_COUNT
    smem = pl.BlockSpec(memory_space=pltpu.SMEM)
    anywhere = pl.BlockSpec(memory_space=pl.ANY)
    dma = pltpu.SemaphoreType.DMA
    return pl.pallas_call(
        functools.partial(exchange_kernel, groups, shares, slots),
        out_shape=(
            jax.ShapeDtypeStruct((lead, width), bf16),
            jax.ShapeDtypeStruct((slots, ROWS, ATTN_DIM), bf16),
        ),
        in_specs=[smem] * 2 + [anywhere] * 5,
        out_specs=(pl.BlockSpec(memory_space=pltpu.VMEM), anywhere),
        scratch_shapes=[
            *[pltpu.VMEM((count, ROWS // PARTS, ATTN_DIM), bf16)] * PARTS,
            *[pltpu.VMEM((slots, ROWS // PARTS, ATTN_DIM), bf16)] * PARTS,
            *[pltpu.VMEM((groups * slots, part, ATTN_DIM), bf16)] * PARTS,
            pltpu.VMEM((PARTS * groups * slots, part, ATTN_DIM), bf16),
            pltpu.VMEM(query.shape, bf16),
            pltpu.VMEM(new.shape, bf16),
            pltpu.VMEM(kv.shape, bf16),
            pltpu.VMEM(weight.shape, bf16),
            pltpu.VMEM((lead, weight.shape[0]), bf16),
            pltpu.VMEM((shares, lead, width), bf16),
            pltpu.VMEM((shares - 1, lead, width), bf16),
            dma((PARTS,)),
            dma((4,)),
            dma((PARTS,)),
            dma((PARTS,)),
            dma,
            dma,
            dma,
            dma,
            dma((PARTS,)),
        ],
        compiler_params=pltpu.CompilerParams(
            collective_id=0, has_side_effects=True, vmem_limit_bytes=60 * 1024 * 1024
        ),
        name="exchange",
    )(chosen, lengths, query, new, kv, weight, cache)


def order_kernel(groups, count, slots, source, chosen):
    me = lax.axis_index("cand")
    total = source.shape[1]
    row = source[...]
    owner = lax.div(row, count)
    across = jnp.broadcast_to(owner.astype(jnp.float32), (total, total))
    before = lax.broadcasted_iota(jnp.int32, (total, total), 0) < lax.broadcasted_iota(
        jnp.int32, (total, total), 1
    )
    rank = jnp.where((across == across.T) & before, 1.0, 0.0).sum(0, keepdims=True)
    rank = rank.astype(jnp.int32)
    chosen[0:1, :] = lax.rem(me - owner + groups, groups) * slots + rank
    lane = lax.broadcasted_iota(jnp.int32, row.shape, 1)
    picked = jnp.zeros_like(row)
    local = lax.rem(row, count)
    for k in range(slots):
        one = jnp.where((owner == me) & (rank == k), local, 0).sum(1, keepdims=True)
        picked = jnp.where(lane == k, one, picked)
    chosen[1:2, :] = picked


def order(groups, count, slots, source):
    vmem = pl.BlockSpec(memory_space=pltpu.VMEM)
    return pl.pallas_call(
        functools.partial(order_kernel, groups, count, slots),
        out_shape=jax.ShapeDtypeStruct((2, source.shape[0]), jnp.int32),
        in_specs=[vmem],
        out_specs=vmem,
        name="order",
    )(source.reshape(1, -1))


def policy_kernel(
    source,
    lengths,
    moved,
    reward,
    new,
    query,
    kept,
    out,
    reward_out,
    held,
    passing,
    in_sem,
    out_sem,
    pass_sem,
):
    me = lax.axis_index("cand")
    slots = query.shape[0]
    loads = [pltpu.make_async_copy(moved.at[s], held.at[s], in_sem.at[s]) for s in range(slots)]
    stores = [pltpu.make_async_copy(held.at[s], kept.at[s], out_sem.at[s]) for s in range(slots)]
    for load in loads:
        load.start()
    come = pltpu.make_async_copy(reward, passing, pass_sem.at[0])
    go = pltpu.make_async_copy(passing, reward_out, pass_sem.at[1])
    come.start()
    asked = query[...].astype(jnp.float32)
    fresh = new[...]
    place = lax.broadcasted_iota(jnp.int32, (PER_KV, CACHE_LENGTH), 1)
    tile = 16
    within = lax.broadcasted_iota(jnp.int32, (tile, ATTN_DIM), 0)
    lines = []
    for s in range(slots):
        length = lengths[source[me * slots + s]]
        base = lax.div(length, tile) * tile
        loads[s].wait()
        for half in range(2):
            rows = pl.ds(pl.multiple_of(half * CACHE_LENGTH + base, tile), tile)
            held[s, rows, :] = jnp.where(
                within + base == length, fresh[s, half : half + 1, :], held[s, rows, :]
            )
        heads = jnp.concatenate(
            [asked[s : s + 1, g * ATTN_DIM : (g + 1) * ATTN_DIM] for g in range(PER_KV)], axis=0
        ).astype(jnp.bfloat16)
        found = score(heads, held[s, 0:CACHE_LENGTH, :]) * SCALE
        found = jnp.where(place <= length, found, -1e30)
        found = jnp.exp(found - found.max(-1, keepdims=True))
        found = found * (1.0 / found.sum(-1, keepdims=True))
        mixed = jnp.dot(
            found.astype(jnp.bfloat16),
            held[s, CACHE_LENGTH:ROWS, :],
            preferred_element_type=jnp.float32,
        )
        stores[s].start()
        lines.append(jnp.concatenate([mixed[g : g + 1] for g in range(PER_KV)], axis=1))
        if s == 0:
            come.wait()
            go.start()
    out[...] = jnp.concatenate(lines, axis=0).astype(jnp.bfloat16)
    for store in stores:
        store.wait()
    go.wait()


def policy(source, lengths, moved, reward, new, query):
    slots = query.shape[0]
    bf16 = jnp.bfloat16
    smem = pl.BlockSpec(memory_space=pltpu.SMEM)
    vmem = pl.BlockSpec(memory_space=pltpu.VMEM)
    anywhere = pl.BlockSpec(memory_space=pl.ANY)
    dma = pltpu.SemaphoreType.DMA
    return pl.pallas_call(
        policy_kernel,
        out_shape=(
            jax.ShapeDtypeStruct(moved.shape, bf16),
            jax.ShapeDtypeStruct(query.shape, bf16),
            jax.ShapeDtypeStruct(reward.shape, bf16),
        ),
        in_specs=[smem, smem, anywhere, anywhere, vmem, vmem],
        out_specs=(anywhere, vmem, anywhere),
        scratch_shapes=[
            pltpu.VMEM(moved.shape, bf16),
            pltpu.VMEM(reward.shape, bf16),
            dma((slots,)),
            dma((slots,)),
            dma((2,)),
        ],
        name="policy",
    )(source, lengths, moved, reward, new, query)


def body(
    groups,
    shares,
    reward_query,
    reward_new,
    reward_key_value_cache,
    reward_length,
    out_weight,
    policy_cache,
    policy_length,
    source,
    policy_query,
    policy_new,
):
    count = reward_query.shape[0]
    slots = policy_query.shape[0]
    reward, moved = exchange(
        groups,
        shares,
        slots,
        order(groups, count, slots, source),
        reward_length,
        reward_query,
        reward_new,
        reward_key_value_cache,
        out_weight,
        policy_cache.reshape(count, ROWS, ATTN_DIM),
    )
    compacted, policy_attn, reward_out = policy(
        source, policy_length, moved, reward, policy_new, policy_query
    )
    return (reward_out, compacted.reshape(slots, 2, CACHE_LENGTH, ATTN_DIM), policy_attn)


def solution(mesh):
    in_specs = (
        P("cand", None, "tp"),
        P("cand", None, None, "tp"),
        P("cand", None, None, "tp"),
        P("cand"),
        P("tp", None),
        P("cand", None, None, "tp"),
        P(),
        P(),
        P("cand", "tp"),
        P("cand", None, "tp"),
    )
    out_specs = (P("cand", "tp"), P("cand", None, None, "tp"), P("cand", "tp"))
    return jax.shard_map(
        functools.partial(body, mesh.shape["cand"], mesh.shape["tp"]),
        mesh=mesh,
        in_specs=in_specs,
        out_specs=out_specs,
        check_vma=False,
    )
```

time: 95.3 us -> 89.2 us (0.936)
  other arithmetic: 4.65 us -> 0 us
  local copies, waits for them, and re-layouts: 2.32 us -> 0 us
    select_n x3 -> x0, other arithmetic: 2.65 us -> none  [the longest x2 1.98 us: body(): slot_lengths = jnp.take(policy_length, local_source)]
    unnamed x3 -> x0, local copies, waits for them, and re-layouts: 1.68 us -> none
    pallas_call x1 -> x2, Pallas kernels: 5.26 us -> 6.11 us  [the longest x1 4.68 us: policy(): pl.pallas_call(policy_kernel, out_shape=(jax.ShapeDtypeStruct(moved.shape...]
where the time goes in v3:
time: 89.2 us; the launch traced here: 89 us
  Pallas kernels  88.4 us (99%)
    pallas_call x1, Pallas kernels, exchange(): pl.pallas_call(functools.partial(exchange_kernel, groups, shares, slots),...  82.2 us
    pallas_call x1, Pallas kernels, policy(): pl.pallas_call(policy_kernel, out_shape=(jax.ShapeDtypeStruct(moved.shape...  4.68 us

profile of v3, /device:TPU:32, one launch (start us, length us, event | category | flops | bytes accessed | tf_op | source)
XLA Modules:
  0.0 89.0 jit_solution(10201789591499589910)
XLA Ops:
  0.6 1.4 %order.1.chosen = s32[2,128]{1,0:T(2,128)} custom-call(s32[1,128]{1,0:T(1,128)} %bitcast.4), custom_call_target="tpu_custom_call" | custom-call | tf_op jit(solution)/shard_map/order/pallas_call | solution.py:321
  2.1 82.2 %exchange.1 = (bf16[256,512]{1,0:T(8,128)(2,1)}, bf16[4,1536,128]{2,1,0:T(8,128)(2,1)}) custom-call(s32[2,128]{1,0:T(2,128)} %order.1.chosen, s32[8]{0:T(128)} %lengths.2, bf16[8,32,1024]{2,1,0:T(8,128)(2,1)} %query_hbm.1, bf16[8,2,32,128]{3,2,1,0:T(8,128)(2,1)} %new_hbm.1, bf16[8,2,768,128]{3,2,1,0:T(8,128)(2,1)} %kv_hbm.1, bf16[1024,4096]{1,0:T(8,128)(2,1)} %weight_hbm.1, ...), custom_call_target="tpu_custom_call" | custom-call | tf_op jit(solution)/shard_map/exchange/pallas_call | solution.py:261
  84.3 4.7 %policy.1 = (bf16[4,1536,128]{2,1,0:T(8,128)(2,1)}, bf16[4,1024]{1,0:T(4,128)(2,1)}, bf16[256,512]{1,0:T(8,128)(2,1)}) custom-call(s32[128]{0:T(128)} %source.1, s32[256]{0:T(256)} %lengths.3, bf16[4,1536,128]{2,1,0:T(8,128)(2,1)} %get-tuple-element.8.moved, bf16[256,512]{1,0:T(8,128)(2,1)} %get-tuple-element.9.reward, bf16[4,2,128]{2,1,0:T(2,128)(2,1)} %new.1, ...), custom_call_target="tpu_custom_call" | custom-call | tf_op jit(solution)/shard_map/policy/pallas_call | solution.py:400

commit v4 on v3

--- a/solution.py
+++ b/solution.py
@@ -354,12 +354,13 @@
     come.start()
     asked = query[...].astype(jnp.float32)
     fresh = new[...]
-    place = lax.broadcasted_iota(jnp.int32, (PER_KV, CACHE_LENGTH), 1)
+    place = lax.broadcasted_iota(jnp.int32, (slots * PER_KV, CACHE_LENGTH), 1)
     tile = 16
     within = lax.broadcasted_iota(jnp.int32, (tile, ATTN_DIM), 0)
-    lines = []
+    ends, scores = [], []
     for s in range(slots):
         length = lengths[source[me * slots + s]]
+        ends.append(jnp.full((PER_KV, CACHE_LENGTH), length, jnp.int32))
         base = lax.div(length, tile) * tile
         loads[s].wait()
         for half in range(2):
@@ -370,20 +371,25 @@
         heads = jnp.concatenate(
             [asked[s : s + 1, g * ATTN_DIM : (g + 1) * ATTN_DIM] for g in range(PER_KV)], axis=0
         ).astype(jnp.bfloat16)
-        found = score(heads, held[s, 0:CACHE_LENGTH, :]) * SCALE
-        found = jnp.where(place <= length, found, -1e30)
-        found = jnp.exp(found - found.max(-1, keepdims=True))
-        found = found * (1.0 / found.sum(-1, keepdims=True))
-        mixed = jnp.dot(
-            found.astype(jnp.bfloat16),
-            held[s, CACHE_LENGTH:ROWS, :],
-            preferred_element_type=jnp.float32,
-        )
-        stores[s].start()
-        lines.append(jnp.concatenate([mixed[g : g + 1] for g in range(PER_KV)], axis=1))
+        scores.append(score(heads, held[s, 0:CACHE_LENGTH, :]) * SCALE)
         if s == 0:
             come.wait()
             go.start()
+        if s > 0:
+            stores[s - 1].start()
+    stores[slots - 1].start()
+    found = jnp.concatenate(scores, axis=0)
+    found = jnp.where(place <= jnp.concatenate(ends, axis=0), found, -1e30)
+    found = jnp.exp(found - found.max(-1, keepdims=True))
+    found = (found * (1.0 / found.sum(-1, keepdims=True))).astype(jnp.bfloat16)
+    lines = []
+    for s in range(slots):
+        mixed = jnp.dot(
+            found[s * PER_KV : (s + 1) * PER_KV],
+            held[s, CACHE_LENGTH:ROWS, :],
+            preferred_element_type=jnp.float32,
+        )
+        lines.append(jnp.concatenate([mixed[g : g + 1] for g in range(PER_KV)], axis=1))
     out[...] = jnp.concatenate(lines, axis=0).astype(jnp.bfloat16)
     for store in stores:
         store.wait()

time: 89.2 us -> 88.6 us (level)
  no operation moved by 1% of the time
where the time goes in v4:
time: 88.6 us; the launch traced here: 88.4 us
  Pallas kernels  87.8 us (99%)
    pallas_call x1, Pallas kernels, exchange(): pl.pallas_call(functools.partial(exchange_kernel, groups, shares, slots),...  82.2 us
    pallas_call x1, Pallas kernels, policy(): pl.pallas_call(policy_kernel, out_shape=(jax.ShapeDtypeStruct(moved.shape...  4.12 us

profile of v4, /device:TPU:32, one launch (start us, length us, event | category | flops | bytes accessed | tf_op | source)
XLA Modules:
  0.0 88.4 jit_solution(2640536726775011706)
XLA Ops:
  0.6 1.4 %order.1.chosen = s32[2,128]{1,0:T(2,128)} custom-call(s32[1,128]{1,0:T(1,128)} %bitcast.4), custom_call_target="tpu_custom_call" | custom-call | tf_op jit(solution)/shard_map/order/pallas_call | solution.py:321
  2.1 82.2 %exchange.1 = (bf16[256,512]{1,0:T(8,128)(2,1)}, bf16[4,1536,128]{2,1,0:T(8,128)(2,1)}) custom-call(s32[2,128]{1,0:T(2,128)} %order.1.chosen, s32[8]{0:T(128)} %lengths.2, bf16[8,32,1024]{2,1,0:T(8,128)(2,1)} %query_hbm.1, bf16[8,2,32,128]{3,2,1,0:T(8,128)(2,1)} %new_hbm.1, bf16[8,2,768,128]{3,2,1,0:T(8,128)(2,1)} %kv_hbm.1, bf16[1024,4096]{1,0:T(8,128)(2,1)} %weight_hbm.1, ...), custom_call_target="tpu_custom_call" | custom-call | tf_op jit(solution)/shard_map/exchange/pallas_call | solution.py:261
  84.3 4.1 %policy.1 = (bf16[4,1536,128]{2,1,0:T(8,128)(2,1)}, bf16[4,1024]{1,0:T(4,128)(2,1)}, bf16[256,512]{1,0:T(8,128)(2,1)}) custom-call(s32[128]{0:T(128)} %source.1, s32[256]{0:T(256)} %lengths.3, bf16[4,1536,128]{2,1,0:T(8,128)(2,1)} %get-tuple-element.8.moved, bf16[256,512]{1,0:T(8,128)(2,1)} %get-tuple-element.9.reward, bf16[4,2,128]{2,1,0:T(2,128)(2,1)} %new.1, ...), custom_call_target="tpu_custom_call" | custom-call | tf_op jit(solution)/shard_map/policy/pallas_call | solution.py:406
